TPU v7x, 128 devices: a whole 4x4x4 slice. The times are simulated.
128 devices in a mesh: row: 8 (over x, y_hi), col: 16 (over y_lo, z, core).
Axes of the slice: x: 4, y: 4 (y_hi: 2, y_lo: 2; y = y_hi * 2 + y_lo), z: 4, core: 2. Of those that a mesh axis runs over, the one named last changes fastest.
Arguments:
- front_trailing: float32 [16384, 16384], P('row', 'col'), may hold values from -6 to 6
- panel_columns: float32 [16384, 1024], P('row', 'col'), may hold values from -0.1875 to 0.1875
- panel_rows: float32 [1024, 16384], P('row', 'col'), may hold values from -6 to 6
- pivots: int32 [1024], replicated, may hold values from 0 to 1023, each once
- diag_inverse: float32 [1024, 1024], replicated, may hold values from -0.1875 to 0.1875
- test_matrix: float32 [16384, 512], P('col'), may hold values from -0.046875 to 0.046875
Outputs:
- schur: float32 [16384, 16384], P('row', 'col')
- off_samples: float32 [16384, 512], P(('row', 'col'))
- leaf_blocks: float32 [16384, 128], P(('row', 'col'))
- group_gram: float32 [8, 512, 512], P('row')
Inputs may be any that keep to these rules, and one draw needn't show every extreme that they name: pivots names each of 0 to 1023 once.
All inputs are finite; a program needn't handle non-finite values.
Results may differ from a plain program's by a relative error of at most 0.000084.
Values sent between devices are 32-bit elements; how exact they have to be, the bound alone decides.
A program may use at most 128 MiB of HBM per device.

v0:
```python
import jax
import jax.numpy as jnp
from jax import lax
from jax.sharding import PartitionSpec as P

LEAF = 128


def product(left, right):
    return jnp.dot(left, right, precision=lax.Precision.HIGH, preferred_element_type=jnp.float32)


def body(front_trailing, panel_columns, panel_rows, pivots, diag_inverse, test_matrix):
    col_count = lax.axis_size("col")
    row_count = lax.axis_size("row")
    row_index = lax.axis_index("row")
    col_index = lax.axis_index("col")
    height, width = front_trailing.shape
    upper_full = lax.all_gather(panel_rows, "row", axis=0, tiled=True)
    left = lax.all_gather(panel_columns, "col", axis=1, tiled=True)
    upper = jnp.take(upper_full, pivots, axis=0)
    weight = product(diag_inverse, upper)
    schur = front_trailing - product(left, weight)
    rows = row_index * height + jnp.arange(height, dtype=jnp.int32)
    cols = col_index * width + jnp.arange(width, dtype=jnp.int32)
    same_leaf = rows[:, None] // LEAF == cols[None, :] // LEAF
    masked = jnp.where(same_leaf, jnp.zeros_like(schur), schur)
    partial = product(masked, test_matrix)
    count = width // LEAF
    ratio = col_count // row_count
    leaves = height // LEAF
    kept = []
    for leaf in range(leaves):
        held = col_index == row_index * ratio + leaf // count
        block = schur[
            leaf * LEAF : (leaf + 1) * LEAF, leaf % count * LEAF : (leaf % count + 1) * LEAF
        ]
        kept.append(jnp.where(held, block, jnp.zeros_like(block)))
    both = jnp.concatenate([partial, jnp.concatenate(kept, axis=0)], axis=1)
    own = lax.psum_scatter(both, "col", scatter_dimension=0, tiled=True)
    own_samples = own[:, : partial.shape[1]]
    leaf_blocks = own[:, partial.shape[1] :]
    gram = lax.dot_general(
        own_samples,
        own_samples,
        (((0,), (0,)), ((), ())),
        precision=lax.Precision.HIGH,
        preferred_element_type=jnp.float32,
    )
    gram = lax.psum(gram, "col")
    route = [(i, i ^ 1) for i in range(row_count)]
    gram = gram + lax.ppermute(gram, "row", route)
    group_gram = (gram / (2 * height))[None]
    return (schur, own_samples, leaf_blocks, group_gram)


def solution(mesh):
    placed = (P("row", "col"), P("row", "col"), P("row", "col"), P(), P(), P("col", None))
    return jax.shard_map(
        body,
        mesh=mesh,
        in_specs=placed,
        out_specs=(
            P("row", "col"),
            P(("row", "col"), None),
            P(("row", "col"), None),
            P("row", None, None),
        ),
        check_vma=False,
    )
```

profile of v0, /device:TPU:0, one launch (start us, length us, event | category | flops | bytes accessed | tf_op | source)
XLA Modules:
  0.0 392.7 jit_solution(6487991175751841340)
XLA Ops:
  7.2 0.0 copy-start
  7.2 0.0 all-gather.3.cloned.1.call-start
  7.2 0.7 all-gather.3.cloned.1.call-update
  7.9 0.0 all-gather.5.cloned.1.call-start
  8.0 0.7 all-gather.5.cloned.1.call-update
  8.7 0.0 reduce-scatter.2.cloned.1.call-start
  8.7 0.0 copy-start.3
  8.7 9.1 %copy.10 = f32[2048,1024]{0,1:T(8,128)} copy(f32[2048,1024]{1,0:T(8,128)} %param.6) | data formatting | bytes 16777216 | tf_op args[0]
  17.9 0.0 copy-done.3
  17.9 66.5 %all-gather.3.cloned.1.call-done = f32[1024,1024]{1,0:T(8,128)} async-done(((f32[128,1024]{1,0:T(8,128)}), f32[1024,1024]{1,0:T(8,128)}) %all-gather.3.cloned.1.call-update) | async-done | bytes 4194320 | tf_op jit(solution)/shard_map/all_gather | solution.py:19
  84.4 8.6 %gather_fusion = f32[1024,1024]{1,0:T(8,128)} fusion(f32[1024,1024]{1,0:T(8,128)} %all-gather.3.cloned.1.call-done, s32[1024]{0:T(1024)S(1)} %fusion.32), kind=kCustom, calls=%fused_computation | custom fusion | bytes 8392704 | tf_op jit(solution)/shard_map/jit(_take)/gather | solution.py:21
  93.0 17.9 %fusion.5 = f32[1024,1024]{1,0:T(8,128)} fusion(f32[1024,1024]{1,0:T(8,128)} %param.10, f32[1024,1024]{1,0:T(8,128)} %gather_fusion, pred[1024]{0:T(1024)(128)(4,1)S(1)} %compare_and_fusion), kind=kOutput, calls=%fused_computation.8 | convolution fusion | flops 6443499520 | bytes 12583936 | tf_op jit(solution)/shard_map/dot_general | solution.py:10
  110.9 25.2 %all-gather.5.cloned.1.call-done = f32[2048,1024]{0,1:T(8,128)} async-done(((f32[2048,64]{0,1:T(8,128)}), f32[2048,1024]{0,1:T(8,128)}) %all-gather.5.cloned.1.call-update) | async-done | bytes 8388624 | tf_op jit(solution)/shard_map/all_gather | solution.py:20
  136.1 17.8 %bitcast_subtract_fusion = f32[2048,1024]{0,1:T(8,128)S(1)} fusion(f32[2048,1024]{0,1:T(8,128)} %copy.10, f32[1024,1024]{1,0:T(8,128)} %fusion.5, f32[2048,1024]{0,1:T(8,128)} %all-gather.5.cloned.1.call-done), kind=kOutput, calls=%fused_computation.1 | convolution fusion | flops 12886999040 | bytes 29360128 | tf_op jit(solution)/shard_map/dot_general | solution.py:10
  154.0 0.0 copy-start.1
  154.3 0.0 copy-done
  154.3 7.6 %fusion = f32[2048,512]{0,1:T(8,128)S(1)} fusion(f32[1024,512]{1,0:T(8,128)S(1)} %copy-done, f32[2048,1024]{0,1:T(8,128)S(1)} %bitcast_subtract_fusion, s32[2048]{0:T(1024)S(1)} %add_select_fusion, s32[1024]{0:T(1024)S(1)} %add_select_fusion.1), kind=kOutput, calls=%fused_computation.2 | convolution fusion | flops 6446645248 | bytes 14692352 | tf_op jit(solution)/shard_map/dot_general | solution.py:10
  161.9 3.0 pad_maximum_fusion
  164.9 0.0 reduce-scatter.2.cloned.1.call-update
  164.9 0.0 all-reduce.2.cloned.1.call-start
  165.0 70.5 %reduce-scatter.2.cloned.1.call-done = f32[128,640]{0,1:T(8,128)} async-done(((f32[2048,640]{0,1:T(8,128)}), f32[128,640]{0,1:T(8,128)}) %reduce-scatter.2.cloned.1.call-update) | async-done | bytes 327696 | tf_op jit(solution)/shard_map/reduce_scatter | solution.py:40
  235.5 2.6 fusion.35
  238.1 0.0 all-reduce.2.cloned.1.call-update
  238.1 0.0 slice-start
  238.1 0.0 slice-start.1
  238.1 119.0 %all-reduce.2.cloned.1.call-done = f32[512,512]{1,0:T(8,128)} async-done(((f32[512,512]{1,0:T(8,128)}), f32[512,512]{1,0:T(8,128)}) %all-reduce.2.cloned.1.call-update) | async-done | bytes 1048592 | tf_op jit(solution)/shard_map/psum | solution.py:50
  357.1 2.7 collective-permute-start
  359.8 9.2 %copy.11 = f32[2048,1024]{1,0:T(8,128)} copy(f32[2048,1024]{0,1:T(8,128)} %copy-done.1) | data formatting | bytes 16777216
  369.1 0.8 copy.12
  369.9 0.7 copy.13
  370.6 13.1 %collective-permute-done = f32[512,512]{1,0:T(8,128)} collective-permute-done((f32[512,512]{1,0:T(8,128)}, f32[512,512]{1,0:T(8,128)}, u32[]{:S(2)}, u32[]{:S(2)}) %collective-permute-start) | collective-permute-done | bytes 1048608 | tf_op jit(solution)/shard_map/ppermute | solution.py:52
  383.7 2.4 multiply_bitcast_fusion
  (25 shorter events, 0.2 us)
Async XLA Ops:
  7.2 147.1 %copy-start = (f32[1024,512]{1,0:T(8,128)S(1)}, f32[1024,512]{1,0:T(8,128)}, u32[]{:S(2)}) copy-start(f32[1024,512]{1,0:T(8,128)} %param.11) | copy-start | bytes 6291460
  7.2 77.2 %all-gather.3.cloned.1.call-start = ((), (), s32[]{:S(2)}) async-start(), calls=%async_computation.1 | async-start | bytes 4718592 | tf_op jit(solution)/shard_map/all_gather | solution.py:19
  7.9 128.2 %all-gather.5.cloned.1.call-start = ((), (), s32[]{:S(2)}) async-start(), calls=%async_computation.2 | async-start | bytes 8912896 | tf_op jit(solution)/shard_map/all_gather | solution.py:20
  8.7 226.8 %reduce-scatter.2.cloned.1.call-start = ((), (), s32[]{:S(2)}) async-start(), calls=%async_computation.3 | async-start | bytes 5570560 | tf_op jit(solution)/shard_map/reduce_scatter | solution.py:40
  8.7 9.2 %copy-start.3 = (s32[1024]{0:T(1024)S(1)}, s32[1024]{0:T(1024)}, u32[]{:S(2)}) copy-start(s32[1024]{0:T(1024)} %param.9) | copy-start | bytes 12292
  154.0 7.9 %copy-start.1 = (f32[2048,1024]{0,1:T(8,128)}, f32[2048,1024]{0,1:T(8,128)S(1)}, u32[]{:S(2)}) copy-start(f32[2048,1024]{0,1:T(8,128)S(1)} %bitcast_subtract_fusion) | copy-start | bytes 25165828
  164.9 192.2 %all-reduce.2.cloned.1.call-start = ((), (), s32[]{:S(2)}) async-start(), calls=%async_computation.4 | async-start | bytes 2097152 | tf_op jit(solution)/shard_map/psum | solution.py:50
  238.1 131.0 %slice-start = ((f32[128,640]{0,1:T(8,128)}), f32[128,512]{0,1:T(8,128)S(1)}, s32[]{:S(2)}) async-start(f32[128,640]{0,1:T(8,128)} %reduce-scatter.2.cloned.1.call-done), calls=%async_computation.5 | async-start | bytes 524288 | tf_op jit(solution)/shard_map/slice | solution.py:41
  238.1 131.8 %slice-start.1 = ((f32[128,640]{0,1:T(8,128)}), f32[128,128]{0,1:T(8,128)S(1)}, s32[]{:S(2)}) async-start(f32[128,640]{0,1:T(8,128)} %reduce-scatter.2.cloned.1.call-done), calls=%async_computation.6 | async-start | bytes 131072 | tf_op jit(solution)/shard_map/slice | solution.py:42
  357.1 26.6 %copy-start.2 = (f32[512,512]{1,0:T(8,128)S(1)}, f32[512,512]{1,0:T(8,128)}, u32[]{:S(2)}) copy-start(f32[512,512]{1,0:T(8,128)} %all-reduce.2.cloned.1.call-done) | copy-start | bytes 3145732
  357.1 26.6 %collective-permute-start = (f32[512,512]{1,0:T(8,128)}, f32[512,512]{1,0:T(8,128)}, u32[]{:S(2)}, u32[]{:S(2)}) collective-permute-start(f32[512,512]{1,0:T(8,128)} %all-reduce.2.cloned.1.call-done), channel_id=1, source_target_pairs={{0,16},{16,0},{32,48},{48,32},{64,80},{80,64},{96,112},{112,96},{1... | collective-permute-start | bytes 3145736 | tf_op jit(solution)/shard_map/ppermute | solution.py:52
Sparse Core Ops, SparseCore 0:
  10.3 74.0 all-gather.2
  86.1 49.9 all-gather.4
  165.0 70.3 reduce-scatter.1
  238.4 118.7 all-reduce.1
where the time goes:
time: 393 us
  waiting for transfers between devices  296 us (75%)
  matrix products  45.9 us (12%)
  local copies, waits for them, and re-layouts  28.6 us (7%)
  between operations  14 us (4%)
  other arithmetic  5.64 us (1%)
    psum x1, waiting for transfers between devices, body(): gram = lax.psum(gram, 'col')  119 us
    reduce_scatter x1, waiting for transfers between devices, body(): own = lax.psum_scatter(both, 'col', scatter_dimension=0, tiled=True)  70.5 us
    all_gather x1, waiting for transfers between devices, body(): upper_full = lax.all_gather(panel_rows, 'row', axis=0, tiled=True)  66.5 us
    dot_general x3, matrix products, product(): jnp.dot(left, right, precision=lax.Precision.HIGH, preferred_element_type...  43.3 us
    all_gather x1, waiting for transfers between devices, body(): left = lax.all_gather(panel_columns, 'col', axis=1, tiled=True)  25.2 us
    unnamed x12, local copies, waits for them, and re-layouts  20 us
    ppermute x1, waiting for transfers between devices, body(): gram = gram + lax.ppermute(gram, 'row', route)  13.1 us
    gather x1, local copies, waits for them, and re-layouts, body(): upper = jnp.take(upper_full, pivots, axis=0)  8.63 us
  transfers between devices with their start and end apart: 5, of which 5 were waited for; matrix products, arithmetic and copies ran while one was open for 12% of the time, Pallas kernels for 0%

commit v1 on v0

--- a/solution.py
+++ b/solution.py
@@ -17,7 +17,7 @@
     col_index = lax.axis_index("col")
     height, width = front_trailing.shape
     upper_full = lax.all_gather(panel_rows, "row", axis=0, tiled=True)
-    left = lax.all_gather(panel_columns, "col", axis=1, tiled=True)
+    left = jnp.concatenate(lax.all_gather(panel_columns, "col"), axis=1)
     upper = jnp.take(upper_full, pivots, axis=0)
     weight = product(diag_inverse, upper)
     schur = front_trailing - product(left, weight)

time: 393 us -> 410 us (1.043)
  local copies, waits for them, and re-layouts: 28.6 us -> 45 us
    unnamed x12 -> x17, local copies, waits for them, and re-layouts: 20 us -> 28.2 us
    reshape x0 -> x1, local copies, waits for them, and re-layouts: none -> 8.09 us  [body(): left = jnp.concatenate(lax.all_gather(panel_columns, 'col'), axis=1)]
  transfers between devices with their start and end apart: 5 -> 5, of which waited for: 5 -> 5; matrix products, arithmetic and copies ran while one was open for 12% -> 11% of each run, Pallas kernels for 0% -> 0%
where the time goes in v1:
time: 410 us; the launch traced here: 409 us
  waiting for transfers between devices  296 us (72%)
  matrix products  45.9 us (11%)
  local copies, waits for them, and re-layouts  45 us (11%)
  between operations  14 us (3%)
  other arithmetic  5.64 us (1%)
    psum x1, waiting for transfers between devices, body(): gram = lax.psum(gram, 'col')  119 us
    reduce_scatter x1, waiting for transfers between devices, body(): own = lax.psum_scatter(both, 'col', scatter_dimension=0, tiled=True)  70.6 us
    all_gather x1, waiting for transfers between devices, body(): upper_full = lax.all_gather(panel_rows, 'row', axis=0, tiled=True)  66.5 us
    dot_general x3, matrix products, product(): jnp.dot(left, right, precision=lax.Precision.HIGH, preferred_element_type...  43.3 us
    unnamed x17, local copies, waits for them, and re-layouts  28.2 us
    all_gather x1, waiting for transfers between devices, body(): left = jnp.concatenate(lax.all_gather(panel_columns, 'col'), axis=1)  25.2 us
    ppermute x1, waiting for transfers between devices, body(): gram = gram + lax.ppermute(gram, 'row', route)  13.1 us
    gather x1, local copies, waits for them, and re-layouts, body(): upper = jnp.take(upper_full, pivots, axis=0)  8.63 us
  transfers between devices with their start and end apart: 5, of which 5 were waited for; matrix products, arithmetic and copies ran while one was open for 11% of the time, Pallas kernels for 0%

profile of v1, /device:TPU:0, one launch (start us, length us, event | category | flops | bytes accessed | tf_op | source)
XLA Modules:
  0.0 409.4 jit_solution(7802697801661590909)
XLA Ops:
  7.2 0.0 copy-start
  7.2 0.0 all-gather.4.cloned.1.call-start
  7.2 0.7 all-gather.4.cloned.1.call-update
  7.9 0.0 all-gather.6.cloned.1.call-start
  8.0 0.7 all-gather.6.cloned.1.call-update
  8.7 0.0 reduce-scatter.2.cloned.1.call-start
  8.7 9.1 %copy.19 = f32[2048,1024]{0,1:T(8,128)} copy(f32[2048,1024]{1,0:T(8,128)} %param.6) | data formatting | bytes 16777216 | tf_op args[0]
  17.9 66.5 %all-gather.4.cloned.1.call-done = f32[1024,1024]{1,0:T(8,128)} async-done(((f32[128,1024]{1,0:T(8,128)}), f32[1024,1024]{1,0:T(8,128)}) %all-gather.4.cloned.1.call-update) | async-done | bytes 4194320 | tf_op jit(solution)/shard_map/all_gather | solution.py:19
  84.4 8.6 %gather_fusion = f32[1024,1024]{1,0:T(8,128)} fusion(f32[1024,1024]{1,0:T(8,128)} %all-gather.4.cloned.1.call-done, s32[1024]{0:T(1024)S(1)} %fusion.32), kind=kCustom, calls=%fused_computation | custom fusion | bytes 8392704 | tf_op jit(solution)/shard_map/jit(_take)/gather | solution.py:21
  93.0 17.9 %fusion.5 = f32[1024,1024]{1,0:T(8,128)} fusion(f32[1024,1024]{1,0:T(8,128)} %param.10, f32[1024,1024]{1,0:T(8,128)} %gather_fusion, pred[1024]{0:T(1024)(128)(4,1)S(1)} %compare_and_fusion), kind=kOutput, calls=%fused_computation.8 | convolution fusion | flops 6443499520 | bytes 12583936 | tf_op jit(solution)/shard_map/dot_general | solution.py:10
  110.9 25.2 %all-gather.6.cloned.1.call-done = f32[32768,64]{0,1:T(8,128)} async-done(((f32[2048,64]{0,1:T(8,128)}), f32[32768,64]{0,1:T(8,128)}) %all-gather.6.cloned.1.call-update) | async-done | bytes 8388624 | tf_op jit(solution)/shard_map/all_gather | solution.py:20
  136.1 8.3 %copy.23 = f32[8,8,16,2048]{3,2,1,0:T(8,128)S(1)} copy(f32[8,8,16,2048]{3,1,2,0:T(8,128)} %bitcast.16) | data formatting | bytes 16777216
  144.4 0.0 slice-start.1
  144.4 8.1 %copy.18 = f32[2048,16,64]{0,2,1:T(8,128)} copy(f32[2048,16,64]{0,1,2:T(8,128)S(1)} %bitcast.15) | data formatting | bytes 16777216 | tf_op jit(solution)/shard_map/reshape | solution.py:20
  152.5 0.0 slice-done
  152.5 17.9 %bitcast_subtract_fusion = f32[2048,1024]{0,1:T(8,128)S(1)} fusion(f32[2048,1024]{0,1:T(8,128)S(1)} %bitcast.18, f32[1024,1024]{1,0:T(8,128)} %fusion.5, f32[2048,1024]{0,1:T(8,128)} %bitcast.19), kind=kOutput, calls=%fused_computation.1 | convolution fusion | flops 12886999040 | bytes 29360128 | tf_op jit(solution)/shard_map/dot_general | solution.py:10
  170.7 7.6 %fusion = f32[2048,512]{0,1:T(8,128)S(1)} fusion(f32[1024,512]{1,0:T(8,128)S(1)} %copy-done, f32[2048,1024]{0,1:T(8,128)S(1)} %bitcast_subtract_fusion, s32[2048]{0:T(1024)S(1)} %add_select_fusion, s32[1024]{0:T(1024)S(1)} %add_select_fusion.1), kind=kOutput, calls=%fused_computation.2 | convolution fusion | flops 6446645248 | bytes 14692352 | tf_op jit(solution)/shard_map/dot_general | solution.py:10
  178.3 3.0 pad_maximum_fusion
  181.3 0.0 reduce-scatter.2.cloned.1.call-update
  181.3 0.0 all-reduce.2.cloned.1.call-start
  181.4 70.6 %reduce-scatter.2.cloned.1.call-done = f32[128,640]{0,1:T(8,128)} async-done(((f32[2048,640]{0,1:T(8,128)}), f32[128,640]{0,1:T(8,128)}) %reduce-scatter.2.cloned.1.call-update) | async-done | bytes 327696 | tf_op jit(solution)/shard_map/reduce_scatter | solution.py:40
  252.0 2.6 fusion.35
  254.6 0.0 all-reduce.2.cloned.1.call-update
  254.6 0.0 slice-start.2
  254.6 0.0 slice-start.3
  254.6 119.2 %all-reduce.2.cloned.1.call-done = f32[512,512]{1,0:T(8,128)} async-done(((f32[512,512]{1,0:T(8,128)}), f32[512,512]{1,0:T(8,128)}) %all-reduce.2.cloned.1.call-update) | async-done | bytes 1048592 | tf_op jit(solution)/shard_map/psum | solution.py:50
  373.8 2.7 collective-permute-start
  376.6 9.2 %copy.20 = f32[2048,1024]{1,0:T(8,128)} copy(f32[2048,1024]{0,1:T(8,128)} %copy-done.1) | data formatting | bytes 16777216
  385.8 0.8 copy.21
  386.6 0.7 copy.22
  387.4 13.1 %collective-permute-done = f32[512,512]{1,0:T(8,128)} collective-permute-done((f32[512,512]{1,0:T(8,128)}, f32[512,512]{1,0:T(8,128)}, u32[]{:S(2)}, u32[]{:S(2)}) %collective-permute-start) | collective-permute-done | bytes 1048608 | tf_op jit(solution)/shard_map/ppermute | solution.py:52
  400.5 2.4 multiply_bitcast_fusion
  (32 shorter events, 0.2 us)
Async XLA Ops:
  7.2 163.5 %copy-start = (f32[1024,512]{1,0:T(8,128)S(1)}, f32[1024,512]{1,0:T(8,128)}, u32[]{:S(2)}) copy-start(f32[1024,512]{1,0:T(8,128)} %param.11) | copy-start | bytes 6291460
  7.2 77.2 %all-gather.4.cloned.1.call-start = ((), (), s32[]{:S(2)}) async-start(), calls=%async_computation.1 | async-start | bytes 4718592 | tf_op jit(solution)/shard_map/all_gather | solution.py:19
  7.9 128.2 %all-gather.6.cloned.1.call-start = ((), (), s32[]{:S(2)}) async-start(), calls=%async_computation.4 | async-start | bytes 8912896 | tf_op jit(solution)/shard_map/all_gather | solution.py:20
  8.7 243.3 %reduce-scatter.2.cloned.1.call-start = ((), (), s32[]{:S(2)}) async-start(), calls=%async_computation.2 | async-start | bytes 5570560 | tf_op jit(solution)/shard_map/reduce_scatter | solution.py:40
  8.7 9.2 %copy-start.3 = (s32[1024]{0:T(1024)S(1)}, s32[1024]{0:T(1024)}, u32[]{:S(2)}) copy-start(s32[1024]{0:T(1024)} %param.9) | copy-start | bytes 12292
  136.1 16.4 %slice-start = ((s8[8388608]{0:T(1024)(128)(4,1)}), s8[4194304]{0:T(1024)(128)(4,1)S(1)}, s32[]{:S(2)}) async-start(s8[8388608]{0:T(1024)(128)(4,1)} %bitcast.17), calls=%async_computation.5 | async-start | bytes 8388608
  144.4 8.1 %slice-start.1 = ((s8[8388608]{0:T(1024)(128)(4,1)}), s8[4194304]{0:T(1024)(128)(4,1)S(1)}, s32[]{:S(2)}) async-start(s8[8388608]{0:T(1024)(128)(4,1)} %bitcast.17), calls=%async_computation.6 | async-start | bytes 8388608
  170.4 7.9 %copy-start.1 = (f32[2048,1024]{0,1:T(8,128)}, f32[2048,1024]{0,1:T(8,128)S(1)}, u32[]{:S(2)}) copy-start(f32[2048,1024]{0,1:T(8,128)S(1)} %bitcast_subtract_fusion) | copy-start | bytes 25165828
  181.3 192.5 %all-reduce.2.cloned.1.call-start = ((), (), s32[]{:S(2)}) async-start(), calls=%async_computation.3 | async-start | bytes 2097152 | tf_op jit(solution)/shard_map/psum | solution.py:50
  254.6 131.2 %slice-start.2 = ((f32[128,640]{0,1:T(8,128)}), f32[128,512]{0,1:T(8,128)S(1)}, s32[]{:S(2)}) async-start(f32[128,640]{0,1:T(8,128)} %reduce-scatter.2.cloned.1.call-done), calls=%async_computation.7 | async-start | bytes 524288 | tf_op jit(solution)/shard_map/slice | solution.py:41
  254.6 132.0 %slice-start.3 = ((f32[128,640]{0,1:T(8,128)}), f32[128,128]{0,1:T(8,128)S(1)}, s32[]{:S(2)}) async-start(f32[128,640]{0,1:T(8,128)} %reduce-scatter.2.cloned.1.call-done), calls=%async_computation.8 | async-start | bytes 131072 | tf_op jit(solution)/shard_map/slice | solution.py:42
  373.8 26.6 %copy-start.2 = (f32[512,512]{1,0:T(8,128)S(1)}, f32[512,512]{1,0:T(8,128)}, u32[]{:S(2)}) copy-start(f32[512,512]{1,0:T(8,128)} %all-reduce.2.cloned.1.call-done) | copy-start | bytes 3145732
  373.8 26.6 %collective-permute-start = (f32[512,512]{1,0:T(8,128)}, f32[512,512]{1,0:T(8,128)}, u32[]{:S(2)}, u32[]{:S(2)}) collective-permute-start(f32[512,512]{1,0:T(8,128)} %all-reduce.2.cloned.1.call-done), channel_id=1, source_target_pairs={{0,16},{16,0},{32,48},{48,32},{64,80},{80,64},{96,112},{112,96},{1... | collective-permute-start | bytes 3145736 | tf_op jit(solution)/shard_map/ppermute | solution.py:52
Sparse Core Ops, SparseCore 0:
  10.3 74.0 all-gather.3
  86.1 49.9 all-gather.5
  181.4 70.5 reduce-scatter.1
  254.9 118.8 all-reduce.1
